TPU v7x, 32 devices: a whole 2x2x4 slice. The times are simulated.
32 devices in a mesh: dp: 4 (over y, x), space: 8 (over z, core).
Axes of the slice: x: 2, y: 2, z: 4, core: 2. Of those that a mesh axis runs over, the one named last changes fastest.
Arguments:
- features: bfloat16 [4, 2048, 256], P('dp', 'space'), may hold values from -6 to 6
- neighbours: int32 [4, 27, 2048], P('dp', None, 'space'), may hold values from -1 to 2047, as said below
- parents: int32 [4, 2048], P('dp', 'space'), may hold values from 0 to 511, as said below
- conv_first: bfloat16 [27, 256, 256], replicated, may hold values from -0.078125 to 0.078125
- conv_second: bfloat16 [27, 256, 256], replicated, may hold values from -0.078125 to 0.078125
- gain_first: float32 [256], replicated, may hold values from 0.1 to 1.9
- gain_second: float32 [256], replicated, may hold values from 0.1 to 1.9
- down_weight: bfloat16 [256, 512], replicated, may hold values from -0.375 to 0.375
- cotangent: bfloat16 [4, 512, 512], P('dp', 'space'), may hold values from -6 to 6
Outputs:
- fine_out: bfloat16 [4, 2048, 256], P('dp', 'space')
- coarse: bfloat16 [4, 512, 512], P('dp', 'space')
- down_grad: float32 [256, 512], replicated
Inputs may be any that keep to these rules, and one draw needn't show every extreme that they name: `neighbours`: for a site s of the block [d * 256, (d + 1) * 256), every entry is -1 or lies in [(d - 1) * 256, (d + 2) * 256); entry 13 is s itself. The parents of the sites of the block [d * 256, (d + 1) * 256) never decrease along the block and lie in [d * 64, (d + 2) * 64).
All inputs are finite; a program needn't handle non-finite values.
Results may differ from a plain program's by a relative error of at most 0.0057.
Values may be sent and summed in bfloat16 or wider, within the bound.
A program may use at most 64 MiB of HBM per device.

v0:
```python
import math

import jax
import jax.numpy as jnp
from jax import lax
from jax.sharding import PartitionSpec as P


def extended(cells, sides, width):
    for axis, dim in sides:
        count = lax.axis_size(axis)
        ends = count - 1
        head = lax.slice_in_dim(cells, 0, width, axis=dim)
        tail = lax.slice_in_dim(cells, cells.shape[dim] - width, cells.shape[dim], axis=dim)
        cells = jnp.concatenate(
            [
                lax.ppermute(tail, axis, [(i, (i + 1) % count) for i in range(ends)]),
                cells,
                lax.ppermute(head, axis, [((i + 1) % count, i) for i in range(ends)]),
            ],
            axis=dim,
        )
    return cells


def from_behind(array, axis, by):
    length = lax.axis_size(axis)
    pairs = [(i, i + by) for i in range(length) if 0 <= i + by < length]
    return lax.ppermute(array, axis, pairs)


def convolve(field, tap_lists, weights):
    site_rows = field.shape[1]
    nearby = extended(field, (("space", 1),), site_rows)
    lowest = (lax.axis_index("space") - 1) * site_rows
    lookup = jnp.where(tap_lists < 0, 3 * site_rows, tap_lists - lowest)
    window_ids = jnp.arange(3 * site_rows, dtype=jnp.int32)

    def one_tap(running, inputs):
        rows_now, weight = inputs
        selector = (rows_now[:, :, None] == window_ids[None, None, :]).astype(jnp.bfloat16)
        picked = jnp.einsum(
            "wsr,wrc->wsc", selector, nearby, preferred_element_type=jnp.float32
        ).astype(jnp.bfloat16)
        return (
            running + jnp.einsum("wsc,cd->wsd", picked, weight, preferred_element_type=jnp.float32),
            None,
        )

    start = jnp.zeros((field.shape[0], site_rows, weights.shape[2]), jnp.float32)
    running, _ = lax.scan(one_tap, start, (jnp.moveaxis(lookup, 1, 0), weights))
    return running


def settle(running, gain):
    inverse = lax.rsqrt(jnp.mean(running * running, axis=-1, keepdims=True) + 1e-05)
    return jax.nn.silu(running * inverse * gain)


def body(
    features,
    neighbours,
    parents,
    conv_first,
    conv_second,
    gain_first,
    gain_second,
    down_weight,
    cotangent,
):
    middle = settle(convolve(features, neighbours, conv_first), gain_first).astype(jnp.bfloat16)
    fine_out = (
        features.astype(jnp.float32)
        + settle(convolve(middle, neighbours, conv_second), gain_second)
    ).astype(jnp.bfloat16)
    par_rows = cotangent.shape[1]
    owner_id = lax.axis_index("space")
    world_rows = features.shape[0]
    parent_ids = owner_id * par_rows + jnp.arange(2 * par_rows, dtype=jnp.int32)
    onehot = (parents[:, None, :] == parent_ids[None, :, None]).astype(jnp.bfloat16)
    partial_value = jnp.einsum("wps,wsc->wpc", onehot, fine_out, preferred_element_type=jnp.float32)
    tallies = jnp.sum(onehot.astype(jnp.float32), axis=2)
    moved = from_behind((partial_value[:, par_rows:], tallies[:, par_rows:]), "space", 1)
    parent_sums = partial_value[:, :par_rows] + moved[0]
    counts = tallies[:, :par_rows] + moved[1]
    pooled = (parent_sums / jnp.maximum(counts, 1.0)[:, :, None]).astype(jnp.bfloat16)
    coarse = jnp.einsum(
        "wpc,cd->wpd", pooled, down_weight, preferred_element_type=jnp.float32
    ).astype(jnp.bfloat16)
    local_grad = jnp.einsum("wpc,wpd->cd", pooled, cotangent, preferred_element_type=jnp.float32)
    worlds_all = world_rows * lax.axis_size("dp")
    parents_all = par_rows * lax.axis_size("space")
    down_grad = lax.psum(local_grad, ("dp", "space")) * (1.0 / math.sqrt(worlds_all * parents_all))
    return (fine_out, coarse, down_grad)


def solution(mesh):
    return jax.shard_map(
        body,
        mesh=mesh,
        in_specs=(
            P("dp", "space", None),
            P("dp", None, "space"),
            P("dp", "space"),
            P(),
            P(),
            P(),
            P(),
            P(),
            P("dp", "space", None),
        ),
        out_specs=(P("dp", "space", None), P("dp", "space", None), P()),
        check_vma=False,
    )
```

profile of v0, /device:TPU:0, one launch (start us, length us, event | category | flops | bytes accessed | tf_op | source)
XLA Modules:
  0.0 252.0 jit_solution(10413457237684646482)
XLA Ops:
  7.2 2.5 %collective-permute-start = (bf16[1,256,256]{2,1,0:T(8,128)(2,1)}, bf16[1,256,256]{2,1,0:T(8,128)(2,1)S(1)}, u32[]{:S(2)}, u32[]{:S(2)}) collective-permute-start(bf16[1,256,256]{2,1,0:T(8,128)(2,1)} %param.13), channel_id=1, source_target_pairs={{0,1},{1,2},{2,3},{3,4},{4,5},{5,6},{6,7},{8,9},{9,10},{10,11},{11... | collective-permute-start | bytes 393224 | tf_op jit(solution)/shard_map/ppermute | solution.py:17
  11.9 3.5 %collective-permute-done.1 = bf16[1,256,256]{2,1,0:T(8,128)(2,1)S(1)} collective-permute-done((bf16[1,256,256]{2,1,0:T(8,128)(2,1)}, bf16[1,256,256]{2,1,0:T(8,128)(2,1)S(1)}, u32[]{:S(2)}, u32[]{:S(2)}) %collective-permute-start.1) | collective-permute-done | bytes 131104 | tf_op jit(solution)/shard_map/ppermute | solution.py:19
  16.4 39.3 %while.22 = (s32[]{:T(128)}, f32[1,256,256]{2,1,0:T(8,128)S(1)}, s32[27,1,256]{2,1,0:T(1,128)S(1)}, bf16[1,768,256]{2,1,0:T(8,128)(2,1)S(1)}, bf16[27,256,256]{2,1,0:T(8,128)(2,1)}, /*index=5*/s32[]{:T(128)}, s32[]{:T(128)}) while((s32[]{:T(128)}, f32[1,256,256]{2,1,0:T(8,128)S(1)}, s32[27,1,256]{2,1,0:T(1,128)S(1)}, ...), condition=%wide.region_1.2_spmd.clone, body=%wide.region_0.1_spmd.clone.sunk | while | flops 134610944 | bytes 1052251 | solution.py:51
  17.8 1.4 fusion.50
  19.3 1.4 fusion.50
  20.8 1.4 fusion.50
  22.2 1.4 fusion.50
  25.1 1.4 fusion.50
  26.6 1.4 fusion.50
  28.0 1.4 fusion.50
  29.5 1.4 fusion.50
  31.0 1.4 fusion.50
  32.4 1.4 fusion.50
  33.9 1.4 fusion.50
  35.3 1.4 fusion.50
  39.7 1.4 fusion.50
  41.2 1.4 fusion.50
  42.6 1.4 fusion.50
  44.1 1.4 fusion.50
  45.5 1.4 fusion.50
  47.0 1.4 fusion.50
  48.4 1.4 fusion.50
  49.9 1.4 fusion.50
  52.8 1.4 fusion.50
  56.0 5.5 %collective-permute-start.2 = (bf16[1,256,256]{2,1,0:T(8,128)(2,1)S(1)}, bf16[1,256,256]{2,1,0:T(8,128)(2,1)S(1)}, u32[]{:S(2)}, u32[]{:S(2)}) collective-permute-start(bf16[1,256,256]{2,1,0:T(8,128)(2,1)S(1)} %multiply_convert_fusion), channel_id=1, source_target_pairs={{0,1},{1,2},{2,3},{3,4},{4,5},{5,6},{6,7},{8,9},{9,10},{10,11},{11... | collective-permute-start | bytes 393224 | tf_op jit(solution)/shard_map/ppermute | solution.py:17
  63.0 3.0 %collective-permute-start.5 = (f32[1,64]{1,0:T(1,128)S(1)}, f32[1,64]{1,0:T(1,128)S(1)}, u32[]{:S(2)}, u32[]{:S(2)}) collective-permute-start(f32[1,64]{1,0:T(1,128)S(1)} %slice.15), channel_id=1, source_target_pairs={{0,1},{1,2},{2,3},{3,4},{4,5},{5,6},{6,7},{8,9},{9,10},{10,11},{11... | collective-permute-start | bytes 776 | tf_op jit(solution)/shard_map/ppermute | solution.py:29
  66.2 39.3 %while.23 = (s32[]{:T(128)}, f32[1,256,256]{2,1,0:T(8,128)S(1)}, s32[27,1,256]{2,1,0:T(1,128)S(1)}, bf16[1,768,256]{2,1,0:T(8,128)(2,1)S(1)}, bf16[27,256,256]{2,1,0:T(8,128)(2,1)}, /*index=5*/s32[]{:T(128)}, s32[]{:T(128)}) while((s32[]{:T(128)}, f32[1,256,256]{2,1,0:T(8,128)S(1)}, s32[27,1,256]{2,1,0:T(1,128)S(1)}, ...), condition=%wide.region_4.5_spmd.clone, body=%wide.region_3.4_spmd.clone.sunk | while | flops 134610944 | bytes 1052251 | solution.py:51
  66.2 1.4 fusion.54
  67.7 1.4 fusion.54
  106.1 3.6 %collective-permute-start.4 = (f32[1,64,256]{2,1,0:T(8,128)S(1)}, f32[1,64,256]{2,1,0:T(8,128)S(1)}, u32[]{:S(2)}, u32[]{:S(2)}) collective-permute-start(f32[1,64,256]{2,1,0:T(8,128)S(1)} %slice.17), channel_id=1, source_target_pairs={{0,1},{1,2},{2,3},{3,4},{4,5},{5,6},{6,7},{8,9},{9,10},{10,11},{11... | collective-permute-start | bytes 196616 | tf_op jit(solution)/shard_map/ppermute | solution.py:29
  112.5 130.8 %all-reduce.2.cloned.1.call-done = f32[256,512]{1,0:T(8,128)} async-done(((f32[256,512]{1,0:T(8,128)}), f32[256,512]{1,0:T(8,128)}) %all-reduce.2.cloned.1.call-update) | async-done | bytes 524304 | tf_op jit(solution)/shard_map/psum | solution.py:93
  243.2 1.9 broadcast_multiply_fusion
  (128 shorter events, 52.5 us)
Async XLA Ops:
  7.2 104.5 %copy-start = (bf16[256,512]{1,0:T(8,128)(2,1)S(1)}, bf16[256,512]{1,0:T(8,128)(2,1)}, u32[]{:S(2)}) copy-start(bf16[256,512]{1,0:T(8,128)(2,1)} %param.20) | copy-start | bytes 786436
  7.2 48.7 %copy-start.5 = (f32[256]{0:T(256)S(1)}, f32[256]{0:T(256)}, u32[]{:S(2)}) copy-start(f32[256]{0:T(256)} %param.18) | copy-start | bytes 3076
  7.2 55.6 %copy-start.4 = (s32[1,256]{1,0:T(1,128)S(1)}, s32[1,256]{1,0:T(1,128)}, u32[]{:S(2)}) copy-start(s32[1,256]{1,0:T(1,128)} %param.15) | copy-start | bytes 3076
  7.2 236.0 %all-reduce.2.cloned.1.call-start = ((), (), s32[]{:S(2)}) async-start(), calls=%async_computation | async-start | bytes 1048576 | tf_op jit(solution)/shard_map/psum | solution.py:93
  7.2 4.6 %collective-permute-start = (bf16[1,256,256]{2,1,0:T(8,128)(2,1)}, bf16[1,256,256]{2,1,0:T(8,128)(2,1)S(1)}, u32[]{:S(2)}, u32[]{:S(2)}) collective-permute-start(bf16[1,256,256]{2,1,0:T(8,128)(2,1)} %param.13), channel_id=1, source_target_pairs={{0,1},{1,2},{2,3},{3,4},{4,5},{5,6},{6,7},{8,9},{9,10},{10,11},{11... | collective-permute-start | bytes 393224 | tf_op jit(solution)/shard_map/ppermute | solution.py:17
  9.8 5.6 %collective-permute-start.1 = (bf16[1,256,256]{2,1,0:T(8,128)(2,1)}, bf16[1,256,256]{2,1,0:T(8,128)(2,1)S(1)}, u32[]{:S(2)}, u32[]{:S(2)}) collective-permute-start(bf16[1,256,256]{2,1,0:T(8,128)(2,1)} %param.13), channel_id=1, source_target_pairs={{1,0},{2,1},{3,2},{4,3},{5,4},{6,5},{7,6},{9,8},{10,9},{11,10},{12... | collective-permute-start | bytes 393224 | tf_op jit(solution)/shard_map/ppermute | solution.py:19
  55.7 50.0 %copy-start.2 = (bf16[1,256,256]{2,1,0:T(8,128)(2,1)S(1)}, bf16[1,256,256]{2,1,0:T(8,128)(2,1)}, u32[]{:S(2)}) copy-start(bf16[1,256,256]{2,1,0:T(8,128)(2,1)} %param.13) | copy-start | bytes 393220
  55.7 49.9 %copy-start.6 = (f32[256]{0:T(256)S(1)}, f32[256]{0:T(256)}, u32[]{:S(2)}) copy-start(f32[256]{0:T(256)} %param.19) | copy-start | bytes 3076
  56.0 10.1 %collective-permute-start.2 = (bf16[1,256,256]{2,1,0:T(8,128)(2,1)S(1)}, bf16[1,256,256]{2,1,0:T(8,128)(2,1)S(1)}, u32[]{:S(2)}, u32[]{:S(2)}) collective-permute-start(bf16[1,256,256]{2,1,0:T(8,128)(2,1)S(1)} %multiply_convert_fusion), channel_id=1, source_target_pairs={{0,1},{1,2},{2,3},{3,4},{4,5},{5,6},{6,7},{8,9},{9,10},{10,11},{11... | collective-permute-start | bytes 393224 | tf_op jit(solution)/shard_map/ppermute | solution.py:17
  61.5 4.6 %collective-permute-start.3 = (bf16[1,256,256]{2,1,0:T(8,128)(2,1)S(1)}, bf16[1,256,256]{2,1,0:T(8,128)(2,1)S(1)}, u32[]{:S(2)}, u32[]{:S(2)}) collective-permute-start(bf16[1,256,256]{2,1,0:T(8,128)(2,1)S(1)} %multiply_convert_fusion), channel_id=1, source_target_pairs={{1,0},{2,1},{3,2},{4,3},{5,4},{6,5},{7,6},{9,8},{10,9},{11,10},{12... | collective-permute-start | bytes 393224 | tf_op jit(solution)/shard_map/ppermute | solution.py:19
  63.0 46.6 %collective-permute-start.5 = (f32[1,64]{1,0:T(1,128)S(1)}, f32[1,64]{1,0:T(1,128)S(1)}, u32[]{:S(2)}, u32[]{:S(2)}) collective-permute-start(f32[1,64]{1,0:T(1,128)S(1)} %slice.15), channel_id=1, source_target_pairs={{0,1},{1,2},{2,3},{3,4},{4,5},{5,6},{6,7},{8,9},{9,10},{10,11},{11... | collective-permute-start | bytes 776 | tf_op jit(solution)/shard_map/ppermute | solution.py:29
  66.2 44.4 %copy-start.3 = (bf16[1,64,512]{2,1,0:T(8,128)(2,1)S(1)}, bf16[1,64,512]{2,1,0:T(8,128)(2,1)}, u32[]{:S(2)}) copy-start(bf16[1,64,512]{2,1,0:T(8,128)(2,1)} %param.21) | copy-start | bytes 196612
  105.8 139.3 %copy-start.1 = (bf16[1,256,256]{2,1,0:T(8,128)(2,1)}, bf16[1,256,256]{2,1,0:T(8,128)(2,1)S(1)}, u32[]{:S(2)}) copy-start(bf16[1,256,256]{2,1,0:T(8,128)(2,1)S(1)} %add_convert_fusion) | copy-start | bytes 393220
  106.1 4.4 %collective-permute-start.4 = (f32[1,64,256]{2,1,0:T(8,128)S(1)}, f32[1,64,256]{2,1,0:T(8,128)S(1)}, u32[]{:S(2)}, u32[]{:S(2)}) collective-permute-start(f32[1,64,256]{2,1,0:T(8,128)S(1)} %slice.17), channel_id=1, source_target_pairs={{0,1},{1,2},{2,3},{3,4},{4,5},{5,6},{6,7},{8,9},{9,10},{10,11},{11... | collective-permute-start | bytes 196616 | tf_op jit(solution)/shard_map/ppermute | solution.py:29
Sparse Core Ops, SparseCore 0:
  111.8 131.4 all-reduce.1
where the time goes:
time: 253 us; the launch traced here: 252 us
  waiting for transfers between devices  135 us (53%)
  matrix products  78.4 us (31%)
  starting transfers between devices  17.2 us (7%)
  between operations  14.3 us (6%)
  other arithmetic  4.43 us (2%)
    psum x1, waiting for transfers between devices, body(): lax.psum(local_grad, ('dp', 'space'))  131 us
    dot_general x54, matrix products, one_tap(): jnp.einsum('wsc,cd->wsd', picked, weight, preferred_element_type=jnp.floa...  76.4 us
    ppermute x2, starting transfers between devices, extended(): lax.ppermute(tail, axis, [(i, (i + 1) % count) for i in range(ends)])  8 us
    ppermute x2, starting transfers between devices, from_behind(): return lax.ppermute(array, axis, pairs)  6.59 us
  transfers between devices with their start and end apart: 7, of which 3 were waited for; matrix products, arithmetic and copies ran while one was open for 16% of the time, Pallas kernels for 0%

commit v1 on v0

v1 whole, which is shorter than its diff:
```python
import functools
import math

import jax
import jax.numpy as jnp
from jax import lax
from jax.experimental import pallas as pl
from jax.experimental.pallas import tpu as pltpu
from jax.sharding import PartitionSpec as P

F32 = jnp.float32
BF16 = jnp.bfloat16
MESH = pl.DeviceIdType.MESH


def settle(total, gain):
    inverse = lax.rsqrt(jnp.mean(total * total, axis=-1, keepdims=True) + 1e-05)
    u = total * inverse * gain
    return u / (1.0 + jnp.exp(-u))


def kernel(
    shape,
    features,
    neighbours,
    parents,
    gain_first,
    gain_second,
    first_hbm,
    second_hbm,
    down_hbm,
    cot_hbm,
    fine_out,
    coarse,
    grad,
    window,
    middle,
    select,
    picked,
    first,
    second,
    down,
    cot,
    total,
    sums_out,
    sums_in,
    tally_out,
    tally_in,
    parts,
    landed,
    gathered,
    weight_sem,
    small_sem,
    halo_send,
    halo_recv,
    sum_send,
    sum_recv,
    part_send,
    part_recv,
    all_send,
    all_recv,
):
    n_dp, n_space, taps, group, chunks, stride, scale = shape
    n = n_dp * n_space
    rows = features.shape[0]
    par = cot.shape[0]
    chunk_rows, chunk_cols = parts.shape[1:]
    across = grad.shape[1] // chunk_cols
    me_dp, me = lax.axis_index("dp"), lax.axis_index("space")
    flat = me_dp * n_space + me

    def place(device):
        return (device // n_space, device % n_space)

    barrier = pltpu.get_barrier_semaphore()

    def greet(i, carry):
        pl.semaphore_signal(barrier, inc=1, device_id=place((flat + i) % n), device_id_type=MESH)
        return carry

    lax.fori_loop(1, n, greet, 0)

    span = group * first.shape[1]
    steps = taps // group

    def weight_copy(which, g):
        source, target = ((first_hbm, first), (second_hbm, second))[which]
        cut = pl.ds(g * span, span)
        return pltpu.make_async_copy(source.at[cut], target.at[cut], weight_sem.at[which, g])

    small = [
        pltpu.make_async_copy(down_hbm, down, small_sem.at[0]),
        pltpu.make_async_copy(cot_hbm, cot, small_sem.at[1]),
    ]
    for which in range(2):
        for g in range(steps):
            weight_copy(which, g).start()
    for copy in small:
        copy.start()

    ids = neighbours[...]
    lookup = jnp.where(ids < 0, -1, ids - (me - 1) * rows).astype(F32)
    columns = jnp.transpose(lookup)
    places = lax.broadcasted_iota(jnp.int32, (rows, 3 * rows), 1).astype(F32)
    for t in range(taps):
        hit = columns[:, t : t + 1] == places
        select[t] = jnp.where(hit, 1.0, 0.0).astype(BF16)

    parent_ids = me * par + lax.broadcasted_iota(jnp.int32, (2 * par, rows), 0)
    member = jnp.where(parents[...] == parent_ids, 1.0, 0.0)
    tallies = jnp.sum(member, axis=1, keepdims=True)
    tally_out[...] = jnp.broadcast_to(tallies[par:], tally_out.shape)
    member = member.astype(BF16)

    pl.semaphore_wait(barrier, n - 1)

    has_left, has_right = me > 0, me < n_space - 1

    def halo(buffer, phase, side):
        source = features if buffer is window else buffer.at[pl.ds(rows, rows)]
        return pltpu.make_async_remote_copy(
            src_ref=source,
            dst_ref=buffer.at[pl.ds(2 * rows * (1 - side), rows)],
            send_sem=halo_send.at[phase, side],
            recv_sem=halo_recv.at[phase, side],
            device_id=(me_dp, me + (2 * side - 1)),
            device_id_type=MESH,
        )

    def tally_copy():
        return pltpu.make_async_remote_copy(
            src_ref=tally_out,
            dst_ref=tally_in,
            send_sem=sum_send.at[1],
            recv_sem=sum_recv.at[1],
            device_id=(me_dp, me + 1),
            device_id_type=MESH,
        )

    def sums_copy():
        return pltpu.make_async_remote_copy(
            src_ref=sums_out,
            dst_ref=sums_in,
            send_sem=sum_send.at[0],
            recv_sem=sum_recv.at[0],
            device_id=(me_dp, me + 1),
            device_id_type=MESH,
        )

    def exchange_start(buffer, phase):
        @pl.when(has_left)
        def _():
            halo(buffer, phase, 0).start()

        @pl.when(has_right)
        def _():
            halo(buffer, phase, 1).start()

        @pl.when(jnp.logical_not(has_left))
        def _():
            buffer[:rows] = jnp.zeros((rows, buffer.shape[1]), BF16)

        @pl.when(jnp.logical_not(has_right))
        def _():
            buffer[2 * rows :] = jnp.zeros((rows, buffer.shape[1]), BF16)

    def exchange_wait(buffer, phase):
        @pl.when(has_left)
        def _():
            halo(buffer, phase, 0).wait_send()
            halo(buffer, phase, 1).wait_recv()

        @pl.when(has_right)
        def _():
            halo(buffer, phase, 1).wait_send()
            halo(buffer, phase, 0).wait_recv()

    def convolve(buffer, weights, which):
        total[...] = jnp.zeros_like(total)

        def step(g, carry):
            weight_copy(which, g).wait()
            width = buffer.shape[1]
            for j in range(group):
                picked[:, j * width : (j + 1) * width] = jnp.dot(
                    select[g * group + j], buffer[...], preferred_element_type=F32
                ).astype(BF16)
            total[...] += jnp.dot(
                picked[...], weights[pl.ds(g * span, span), :], preferred_element_type=F32
            )
            return carry

        lax.fori_loop(0, steps, step, 0)
        return total[...]

    exchange_start(window, 0)

    @pl.when(has_right)
    def _():
        tally_copy().start()

    @pl.when(jnp.logical_not(has_left))
    def _():
        tally_in[...] = jnp.zeros_like(tally_in)
        sums_in[...] = jnp.zeros_like(sums_in)

    window[rows : 2 * rows] = features[...]
    exchange_wait(window, 0)
    middle[rows : 2 * rows] = settle(convolve(window, first, 0), gain_first[...]).astype(BF16)
    exchange_start(middle, 1)
    exchange_wait(middle, 1)
    fine = (features[...].astype(F32) + settle(convolve(middle, second, 1), gain_second[...])).astype(BF16)
    fine_out[...] = fine

    partial = jnp.dot(member, fine, preferred_element_type=F32)
    sums_out[...] = partial[par:]

    @pl.when(has_right)
    def _():
        sums_copy().start()

    for copy in small:
        copy.wait()

    @pl.when(has_right)
    def _():
        tally_copy().wait_send()
        sums_copy().wait_send()

    @pl.when(has_left)
    def _():
        tally_copy().wait_recv()
        sums_copy().wait_recv()

    counts = tallies[:par] + tally_in[:, :1]
    pooled = ((partial[:par] + sums_in[...]) / jnp.maximum(counts, 1.0)).astype(BF16)
    local = lax.dot_general(
        pooled, cot[...], (((0,), (0,)), ((), ())), preferred_element_type=F32
    )
    for k in range(chunks):
        r, c = (k // across) * chunk_rows, (k % across) * chunk_cols
        parts[k] = local[r : r + chunk_rows, c : c + chunk_cols].astype(BF16)

    mine = flat // stride
    owns = flat % stride == 0

    def part_copy(i):
        k = (mine + i) % chunks
        owner = k * stride
        return owner, pltpu.make_async_remote_copy(
            src_ref=parts.at[k],
            dst_ref=landed.at[(flat - owner - 1 + n) % n],
            send_sem=part_send,
            recv_sem=part_recv,
            device_id=place(owner),
            device_id_type=MESH,
        )

    def send_part(i, carry):
        part_copy(i)[1].start()
        return carry

    lax.fori_loop(1, chunks, send_part, 0)
    if stride > 1:

        @pl.when(jnp.logical_not(owns))
        def _():
            send_part(0, 0)

    coarse[...] = jnp.dot(pooled, down[...], preferred_element_type=F32).astype(BF16)

    def bulk(ref, count, send, recv):
        cut = ref.at[pl.ds(0, count)]
        return pltpu.make_async_remote_copy(
            src_ref=cut,
            dst_ref=cut,
            send_sem=send,
            recv_sem=recv,
            device_id=place((flat + 1) % n),
            device_id_type=MESH,
        )

    def share(i, carry):
        pltpu.make_async_remote_copy(
            src_ref=gathered.at[mine],
            dst_ref=gathered.at[mine],
            send_sem=all_send,
            recv_sem=all_recv,
            device_id=place((flat + i) % n),
            device_id_type=MESH,
        ).start()
        return carry

    def own():
        bulk(landed, n - 1, part_send, part_recv).wait_recv()
        mean = parts[mine].astype(F32)

        def add(i, running):
            return running + landed[i].astype(F32)

        mean = lax.fori_loop(0, n - 1, add, mean, unroll=True)
        gathered[mine] = (mean * scale).astype(BF16)
        lax.fori_loop(1, n, share, 0)
        bulk(parts, chunks - 1, part_send, part_recv).wait_send()
        bulk(gathered, chunks - 1, all_send, all_recv).wait_recv()
        bulk(landed, n - 1, all_send, all_recv).wait_send()

    def follow():
        bulk(parts, chunks, part_send, part_recv).wait_send()
        bulk(gathered, chunks, all_send, all_recv).wait_recv()

    if stride == 1:
        own()
    else:
        pl.when(owns)(own)
        pl.when(jnp.logical_not(owns))(follow)

    for k in range(chunks):
        r, c = (k // across) * chunk_rows, (k % across) * chunk_cols
        grad[r : r + chunk_rows, c : c + chunk_cols] = gathered[k]


def body(
    n_dp,
    n_space,
    features,
    neighbours,
    parents,
    conv_first,
    conv_second,
    gain_first,
    gain_second,
    down_weight,
    cotangent,
):
    worlds, rows, width = features.shape
    taps = neighbours.shape[1]
    par, out_width = cotangent.shape[1:]
    n = n_dp * n_space
    group = 9 if taps % 9 == 0 else 1
    chunks = min(n, (width // 16) * (out_width // 128))
    stride = n // chunks
    tall = min(chunks, width // 16)
    chunk_rows, chunk_cols = width // tall, out_width // (chunks // tall)
    scale = 1.0 / math.sqrt(worlds * n_dp * par * n_space)
    vmem = pl.BlockSpec(memory_space=pltpu.VMEM)
    hbm = pl.BlockSpec(memory_space=pl.ANY)
    dma = pltpu.SemaphoreType.DMA
    fine_out, coarse, grad = pl.pallas_call(
        functools.partial(kernel, (n_dp, n_space, taps, group, chunks, stride, scale)),
        out_shape=(
            jax.ShapeDtypeStruct((rows, width), BF16),
            jax.ShapeDtypeStruct((par, out_width), BF16),
            jax.ShapeDtypeStruct((width, out_width), BF16),
        ),
        in_specs=[vmem] * 5 + [hbm] * 4,
        out_specs=(vmem,) * 3,
        scratch_shapes=[
            pltpu.VMEM((3 * rows, width), BF16),
            pltpu.VMEM((3 * rows, width), BF16),
            pltpu.VMEM((taps, rows, 3 * rows), BF16),
            pltpu.VMEM((rows, group * width), BF16),
            pltpu.VMEM((taps * width, width), BF16),
            pltpu.VMEM((taps * width, width), BF16),
            pltpu.VMEM((width, out_width), BF16),
            pltpu.VMEM((par, out_width), BF16),
            pltpu.VMEM((rows, width), F32),
            pltpu.VMEM((par, width), F32),
            pltpu.VMEM((par, width), F32),
            pltpu.VMEM((par, 128), F32),
            pltpu.VMEM((par, 128), F32),
            pltpu.VMEM((chunks, chunk_rows, chunk_cols), BF16),
            pltpu.VMEM((n - 1, chunk_rows, chunk_cols), BF16),
            pltpu.VMEM((chunks, chunk_rows, chunk_cols), BF16),
            dma((2, taps // group)),
            dma((2,)),
            dma((2, 2)),
            dma((2, 2)),
            dma((2,)),
            dma((2,)),
            dma,
            dma,
            dma,
            dma,
        ],
        compiler_params=pltpu.CompilerParams(
            collective_id=0, has_side_effects=True, vmem_limit_bytes=60 * 2**20
        ),
    )(
        features[0],
        neighbours[0],
        parents,
        gain_first[None],
        gain_second[None],
        conv_first.reshape(taps * width, width),
        conv_second.reshape(taps * width, width),
        down_weight,
        cotangent[0],
    )
    return fine_out[None], coarse[None], grad.astype(F32)


def solution(mesh):
    return jax.shard_map(
        functools.partial(body, mesh.shape["dp"], mesh.shape["space"]),
        mesh=mesh,
        in_specs=(
            P("dp", "space", None),
            P("dp", None, "space"),
            P("dp", "space"),
            P(),
            P(),
            P(),
            P(),
            P(),
            P("dp", "space", None),
        ),
        out_specs=(P("dp", "space", None), P("dp", "space", None), P()),
        check_vma=False,
    )
```

time: 253 us -> 49 us (0.19)
  waiting for transfers between devices: 135 us -> 0 us
  matrix products: 78.4 us -> 0 us
  Pallas kernels: 0 us -> 41.9 us
  starting transfers between devices: 17.2 us -> 0 us
  between operations: 14.3 us -> 0.64 us
  local copies, waits for them, and re-layouts: 0.52 us -> 4.4 us
  other arithmetic: 4.43 us -> 1.8 us
    psum x1 -> x0, waiting for transfers between devices: 131 us -> none  [body(): lax.psum(local_grad, ('dp', 'space'))]
    dot_general x57 -> x0, matrix products: 78.4 us -> none  [the longest x54 76.4 us: one_tap(): jnp.einsum('wsc,cd->wsd', picked, weight, preferred_element_type=jnp.floa...]
    pallas_call x0 -> x1, Pallas kernels: none -> 41.9 us  [body(): pl.pallas_call(functools.partial(kernel, (n_dp, n_space, taps, group, chu...]
    ppermute x6 -> x0, starting transfers between devices: 17.2 us -> none  [the longest x2 8 us: extended(): lax.ppermute(tail, axis, [(i, (i + 1) % count) for i in range(ends)])]
    ppermute x6 -> x0, waiting for transfers between devices: 4.39 us -> none  [the longest x2 3.52 us: extended(): lax.ppermute(head, axis, [((i + 1) % count, i) for i in range(ends)])]
    unnamed x14 -> x3, local copies, waits for them, and re-layouts: 0.04 us -> 4.4 us
  transfers between devices with their start and end apart: 7 -> 0, of which waited for: 3 -> 0; matrix products, arithmetic and copies ran while one was open for 16% -> 0% of each run, Pallas kernels for 0% -> 0%
where the time goes in v1:
time: 49 us; the launch traced here: 48.7 us
  Pallas kernels  41.9 us (86%)
  local copies, waits for them, and re-layouts  4.4 us (9%)
  other arithmetic  1.8 us (4%)
  between operations  0.64 us (1%)
    pallas_call x1, Pallas kernels, body(): pl.pallas_call(functools.partial(kernel, (n_dp, n_space, taps, group, chu...  41.9 us
    unnamed x3, local copies, waits for them, and re-layouts  4.4 us
    convert_element_type x1, other arithmetic, body(): return (fine_out[None], coarse[None], grad.astype(F32))  1.8 us

profile of v1, /device:TPU:0, one launch (start us, length us, event | category | flops | bytes accessed | tf_op | source)
XLA Modules:
  0.0 48.7 jit_solution(11885300749414969653)
XLA Ops:
  0.6 1.4 %copy.14 = s32[1,27,256]{2,1,0:T(8,128)} copy(s32[1,27,256]{2,0,1:T(1,128)} %param.10) | data formatting | bytes 55296
  2.0 41.9 %shard_map.112 = (bf16[256,256]{1,0:T(8,128)(2,1)}, bf16[64,512]{1,0:T(8,128)(2,1)}, bf16[256,512]{1,0:T(8,128)(2,1)}) custom-call(bf16[256,256]{1,0:T(8,128)(2,1)} %bitcast.13, s32[27,256]{1,0:T(8,128)} %bitcast.14, s32[1,256]{1,0:T(1,128)} %parents.1, f32[1,256]{1,0:T(1,128)} %bitcast.18, f32[1,256]{1,0:T(1,128)} %bitcast.19, bf16[6912,256]{1,0:T(8,128)(2,1)} %bitcast.11, ...), custom_call_target="tpu_custom_call" | custom-call | tf_op jit(solution)/shard_map/pallas_call | solution.py:349
  43.9 1.8 %convert_element_type.3 = f32[256,512]{1,0:T(8,128)} convert(bf16[256,512]{1,0:T(8,128)(2,1)} %get-tuple-element.8) | non-fusion elementwise | flops 131072 | bytes 786432 | tf_op jit(solution)/shard_map/convert_element_type | solution.py:400
  45.7 1.6 %copy.17 = bf16[1,256,256]{2,1,0:T(8,128)(2,1)} copy(bf16[1,256,256]{2,1,0:T(8,128)(2,1)} %bitcast.15) | data formatting | bytes 262144
  47.2 1.5 %copy.18 = bf16[1,64,512]{2,1,0:T(8,128)(2,1)} copy(bf16[1,64,512]{2,1,0:T(8,128)(2,1)} %bitcast.17) | data formatting | bytes 131072

commit v2 on v1

--- a/solution.py
+++ b/solution.py
@@ -30,9 +30,9 @@
     second_hbm,
     down_hbm,
     cot_hbm,
-    fine_out,
-    coarse,
-    grad,
+    fine_hbm,
+    coarse_hbm,
+    grad_hbm,
     window,
     middle,
     select,
@@ -42,6 +42,8 @@
     down,
     cot,
     total,
+    fine_out,
+    coarse,
     sums_out,
     sums_in,
     tally_out,
@@ -59,13 +61,15 @@
     part_recv,
     all_send,
     all_recv,
+    out_sem,
 ):
     n_dp, n_space, taps, group, chunks, stride, scale = shape
     n = n_dp * n_space
     rows = features.shape[0]
-    par = cot.shape[0]
+    par = cot.shape[0] // 2
     chunk_rows, chunk_cols = parts.shape[1:]
-    across = grad.shape[1] // chunk_cols
+    across = cot.shape[1] // chunk_cols
+    width = features.shape[1]
     me_dp, me = lax.axis_index("dp"), lax.axis_index("space")
     flat = me_dp * n_space + me
 
@@ -90,15 +94,15 @@
 
     small = [
         pltpu.make_async_copy(down_hbm, down, small_sem.at[0]),
-        pltpu.make_async_copy(cot_hbm, cot, small_sem.at[1]),
+        pltpu.make_async_copy(cot_hbm, cot.at[pl.ds(0, par)], small_sem.at[1]),
     ]
+    for copy in small:
+        copy.start()
     for which in range(2):
         for g in range(steps):
             weight_copy(which, g).start()
-    for copy in small:
-        copy.start()
-
-    ids = neighbours[...]
+
+    ids = neighbours[:, 0, :]
     lookup = jnp.where(ids < 0, -1, ids - (me - 1) * rows).astype(F32)
     columns = jnp.transpose(lookup)
     places = lax.broadcasted_iota(jnp.int32, (rows, 3 * rows), 1).astype(F32)
@@ -109,7 +113,7 @@
     parent_ids = me * par + lax.broadcasted_iota(jnp.int32, (2 * par, rows), 0)
     member = jnp.where(parents[...] == parent_ids, 1.0, 0.0)
     tallies = jnp.sum(member, axis=1, keepdims=True)
-    tally_out[...] = jnp.broadcast_to(tallies[par:], tally_out.shape)
+    tally_out[...] = jnp.broadcast_to(tallies, tally_out.shape)
     member = member.astype(BF16)
 
     pl.semaphore_wait(barrier, n - 1)
@@ -127,25 +131,29 @@
             device_id_type=MESH,
         )
 
-    def tally_copy():
+    def to_side(source, target, slot, side):
         return pltpu.make_async_remote_copy(
-            src_ref=tally_out,
-            dst_ref=tally_in,
-            send_sem=sum_send.at[1],
-            recv_sem=sum_recv.at[1],
-            device_id=(me_dp, me + 1),
+            src_ref=source,
+            dst_ref=target,
+            send_sem=sum_send.at[slot],
+            recv_sem=sum_recv.at[slot],
+            device_id=(me_dp, me + (2 * side - 1)),
             device_id_type=MESH,
         )
 
+    low, high = pl.ds(0, par), pl.ds(par, par)
+
     def sums_copy():
-        return pltpu.make_async_remote_copy(
-            src_ref=sums_out,
-            dst_ref=sums_in,
-            send_sem=sum_send.at[0],
-            recv_sem=sum_recv.at[0],
-            device_id=(me_dp, me + 1),
-            device_id_type=MESH,
-        )
+        return to_side(sums_out, sums_in, 0, 1)
+
+    def count_right():
+        return to_side(tally_out.at[high], tally_in.at[low], 1, 1)
+
+    def count_left():
+        return to_side(tally_out.at[low], tally_in.at[high], 2, 0)
+
+    def cot_left():
+        return to_side(cot.at[low], cot.at[high], 3, 0)
 
     def exchange_start(buffer, phase):
         @pl.when(has_left)
@@ -164,78 +172,124 @@
         def _():
             buffer[2 * rows :] = jnp.zeros((rows, buffer.shape[1]), BF16)
 
-    def exchange_wait(buffer, phase):
-        @pl.when(has_left)
-        def _():
-            halo(buffer, phase, 0).wait_send()
-            halo(buffer, phase, 1).wait_recv()
-
-        @pl.when(has_right)
-        def _():
-            halo(buffer, phase, 1).wait_send()
-            halo(buffer, phase, 0).wait_recv()
+    def arrive(phase, buffer, side):
+        @pl.when((has_right, has_left)[side])
+        def _():
+            halo(buffer, phase, side).wait_recv()
+
+    def sent(phase, buffer):
+        for side, there in enumerate((has_left, has_right)):
+
+            @pl.when(there)
+            def _():
+                halo(buffer, phase, side).wait_send()
+
+    odd = me % 2
 
     def convolve(buffer, weights, which):
+        def pick(stage, g):
+            for j in range(group):
+                spot = (rows, 2 * rows * (1 - odd), 2 * rows * odd)[stage]
+                if stage:
+                    spot = pl.multiple_of(spot, rows)
+                t = g * group + j
+                found = jnp.dot(
+                    select[t, :, pl.ds(spot, rows)],
+                    buffer[pl.ds(spot, rows), :],
+                    preferred_element_type=F32,
+                ).astype(BF16)
+                cut = (g, slice(None), slice(j * width, (j + 1) * width))
+                picked[cut] = picked[cut] + found if stage else found
+
+        def early(stage):
+            def step(g, carry):
+                pick(stage, g)
+                return carry
+
+            lax.fori_loop(0, steps, step, 0)
+
+        early(0)
+
+        @pl.when(odd == 0)
+        def _():
+            arrive(which, buffer, 0)
+
+        @pl.when(odd == 1)
+        def _():
+            arrive(which, buffer, 1)
+
+        early(1)
+
+        @pl.when(odd == 0)
+        def _():
+            arrive(which, buffer, 1)
+
+        @pl.when(odd == 1)
+        def _():
+            arrive(which, buffer, 0)
+
         total[...] = jnp.zeros_like(total)
 
         def step(g, carry):
+            pick(2, g)
             weight_copy(which, g).wait()
-            width = buffer.shape[1]
-            for j in range(group):
-                picked[:, j * width : (j + 1) * width] = jnp.dot(
-                    select[g * group + j], buffer[...], preferred_element_type=F32
-                ).astype(BF16)
             total[...] += jnp.dot(
-                picked[...], weights[pl.ds(g * span, span), :], preferred_element_type=F32
+                picked[g], weights[pl.ds(g * span, span), :], preferred_element_type=F32
             )
             return carry
 
         lax.fori_loop(0, steps, step, 0)
+        sent(which, buffer)
         return total[...]
 
+    window[rows : 2 * rows] = features[...]
     exchange_start(window, 0)
+    for copy in small:
+        copy.wait()
+
+    @pl.when(has_left)
+    def _():
+        count_left().start()
+        cot_left().start()
 
     @pl.when(has_right)
     def _():
-        tally_copy().start()
+        count_right().start()
 
     @pl.when(jnp.logical_not(has_left))
     def _():
-        tally_in[...] = jnp.zeros_like(tally_in)
+        tally_in[:par] = jnp.zeros((par, tally_in.shape[1]), F32)
         sums_in[...] = jnp.zeros_like(sums_in)
 
-    window[rows : 2 * rows] = features[...]
-    exchange_wait(window, 0)
+    @pl.when(jnp.logical_not(has_right))
+    def _():
+        tally_in[par:] = jnp.zeros((par, tally_in.shape[1]), F32)
+        cot[par:] = jnp.zeros((par, cot.shape[1]), BF16)
+
     middle[rows : 2 * rows] = settle(convolve(window, first, 0), gain_first[...]).astype(BF16)
     exchange_start(middle, 1)
-    exchange_wait(middle, 1)
+
+    @pl.when(has_left)
+    def _():
+        count_left().wait_send()
+        cot_left().wait_send()
+        count_right().wait_recv()
+
+    @pl.when(has_right)
+    def _():
+        count_right().wait_send()
+        count_left().wait_recv()
+        cot_left().wait_recv()
+
+    share_of = 1.0 / jnp.maximum(tallies + tally_in[:, :1], 1.0)
     fine = (features[...].astype(F32) + settle(convolve(middle, second, 1), gain_second[...])).astype(BF16)
     fine_out[...] = fine
-
     partial = jnp.dot(member, fine, preferred_element_type=F32)
-    sums_out[...] = partial[par:]
-
-    @pl.when(has_right)
-    def _():
-        sums_copy().start()
-
-    for copy in small:
-        copy.wait()
-
-    @pl.when(has_right)
-    def _():
-        tally_copy().wait_send()
-        sums_copy().wait_send()
-
-    @pl.when(has_left)
-    def _():
-        tally_copy().wait_recv()
-        sums_copy().wait_recv()
-
-    counts = tallies[:par] + tally_in[:, :1]
-    pooled = ((partial[:par] + sums_in[...]) / jnp.maximum(counts, 1.0)).astype(BF16)
     local = lax.dot_general(
-        pooled, cot[...], (((0,), (0,)), ((), ())), preferred_element_type=F32
+        (partial * share_of).astype(BF16),
+        cot[...],
+        (((0,), (0,)), ((), ())),
+        preferred_element_type=F32,
     )
     for k in range(chunks):
         r, c = (k // across) * chunk_rows, (k % across) * chunk_cols
@@ -267,7 +321,25 @@
         def _():
             send_part(0, 0)
 
+    outs = [
+        pltpu.make_async_copy(fine_out, fine_hbm, out_sem.at[0]),
+        pltpu.make_async_copy(coarse, coarse_hbm, out_sem.at[1]),
+    ]
+    outs[0].start()
+    sums_out[...] = partial[par:]
+
+    @pl.when(has_right)
+    def _():
+        sums_copy().start()
+        sums_copy().wait_send()
+
+    @pl.when(has_left)
+    def _():
+        sums_copy().wait_recv()
+
+    pooled = ((partial[:par] + sums_in[...]) * share_of[:par]).astype(BF16)
     coarse[...] = jnp.dot(pooled, down[...], preferred_element_type=F32).astype(BF16)
+    outs[1].start()
 
     def bulk(ref, count, send, recv):
         cut = ref.at[pl.ds(0, count)]
@@ -315,9 +387,21 @@
         pl.when(owns)(own)
         pl.when(jnp.logical_not(owns))(follow)
 
+    last = pltpu.make_async_copy(gathered, grad_hbm, out_sem.at[2])
+    last.start()
+    for copy in outs:
+        copy.wait()
+    last.wait()
+
+
+def finish(fine, coarse, gathered, fine_out, coarse_out, grad):
+    chunks, chunk_rows, chunk_cols = gathered.shape
+    across = grad.shape[1] // chunk_cols
+    fine_out[...] = fine[...]
+    coarse_out[...] = coarse[...]
     for k in range(chunks):
         r, c = (k // across) * chunk_rows, (k % across) * chunk_cols
-        grad[r : r + chunk_rows, c : c + chunk_cols] = gathered[k]
+        grad[r : r + chunk_rows, c : c + chunk_cols] = gathered[k].astype(F32)
 
 
 def body(
@@ -351,24 +435,26 @@
         out_shape=(
             jax.ShapeDtypeStruct((rows, width), BF16),
             jax.ShapeDtypeStruct((par, out_width), BF16),
-            jax.ShapeDtypeStruct((width, out_width), BF16),
+            jax.ShapeDtypeStruct((chunks, chunk_rows, chunk_cols), BF16),
         ),
         in_specs=[vmem] * 5 + [hbm] * 4,
-        out_specs=(vmem,) * 3,
+        out_specs=(hbm,) * 3,
         scratch_shapes=[
             pltpu.VMEM((3 * rows, width), BF16),
             pltpu.VMEM((3 * rows, width), BF16),
             pltpu.VMEM((taps, rows, 3 * rows), BF16),
-            pltpu.VMEM((rows, group * width), BF16),
+            pltpu.VMEM((taps // group, rows, group * width), BF16),
             pltpu.VMEM((taps * width, width), BF16),
             pltpu.VMEM((taps * width, width), BF16),
             pltpu.VMEM((width, out_width), BF16),
+            pltpu.VMEM((2 * par, out_width), BF16),
+            pltpu.VMEM((rows, width), F32),
+            pltpu.VMEM((rows, width), BF16),
             pltpu.VMEM((par, out_width), BF16),
-            pltpu.VMEM((rows, width), F32),
             pltpu.VMEM((par, width), F32),
             pltpu.VMEM((par, width), F32),
-            pltpu.VMEM((par, 128), F32),
-            pltpu.VMEM((par, 128), F32),
+            pltpu.VMEM((2 * par, 128), F32),
+            pltpu.VMEM((2 * par, 128), F32),
             pltpu.VMEM((chunks, chunk_rows, chunk_cols), BF16),
             pltpu.VMEM((n - 1, chunk_rows, chunk_cols), BF16),
             pltpu.VMEM((chunks, chunk_rows, chunk_cols), BF16),
@@ -376,19 +462,20 @@
             dma((2,)),
             dma((2, 2)),
             dma((2, 2)),
-            dma((2,)),
-            dma((2,)),
+            dma((4,)),
+            dma((4,)),
             dma,
             dma,
             dma,
             dma,
+            dma((3,)),
         ],
         compiler_params=pltpu.CompilerParams(
             collective_id=0, has_side_effects=True, vmem_limit_bytes=60 * 2**20
         ),
     )(
         features[0],
-        neighbours[0],
+        jnp.transpose(neighbours, (1, 0, 2)),
         parents,
         gain_first[None],
         gain_second[None],
@@ -397,7 +484,17 @@
         down_weight,
         cotangent[0],
     )
-    return fine_out[None], coarse[None], grad.astype(F32)
+    fine_out, coarse, grad = pl.pallas_call(
+        finish,
+        out_shape=(
+            jax.ShapeDtypeStruct((rows, width), BF16),
+            jax.ShapeDtypeStruct((par, out_width), BF16),
+            jax.ShapeDtypeStruct((width, out_width), F32),
+        ),
+        in_specs=[vmem] * 3,
+        out_specs=(vmem,) * 3,
+    )(fine_out, coarse, grad)
+    return fine_out[None], coarse[None], grad
 
 
 def solution(mesh):

time: 49 us -> 44.1 us (0.900)
  local copies, waits for them, and re-layouts: 4.4 us -> 0 us
  other arithmetic: 1.8 us -> 0 us
  Pallas kernels: 41.9 us -> 43.3 us
    unnamed x3 -> x0, local copies, waits for them, and re-layouts: 4.4 us -> none
    pallas_call x0 -> x1, Pallas kernels: none -> 1.92 us  [body(): pl.pallas_call(finish, out_shape=(jax.ShapeDtypeStruct((rows, width), BF1...]
    convert_element_type x1 -> x0, other arithmetic: 1.8 us -> none  [body(): return (fine_out[None], coarse[None], grad.astype(F32))]
    pallas_call x1, Pallas kernels: 41.9 us -> 41.3 us  [body(): pl.pallas_call(functools.partial(kernel, (n_dp, n_space, taps, group, chu...]
where the time goes in v2:
time: 44.1 us; the launch traced here: 43.9 us
  Pallas kernels  43.3 us (98%)
  between operations  0.64 us (1%)
    pallas_call x1, Pallas kernels, body(): pl.pallas_call(functools.partial(kernel, (n_dp, n_space, taps, group, chu...  41.3 us
    pallas_call x1, Pallas kernels, body(): pl.pallas_call(finish, out_shape=(jax.ShapeDtypeStruct((rows, width), BF1...  1.92 us

profile of v2, /device:TPU:0, one launch (start us, length us, event | category | flops | bytes accessed | tf_op | source)
XLA Modules:
  0.0 43.9 jit_solution(4644262663892625648)
XLA Ops:
  0.6 41.3 %shard_map.112 = (bf16[256,256]{1,0:T(8,128)(2,1)}, bf16[64,512]{1,0:T(8,128)(2,1)}, bf16[32,16,256]{2,1,0:T(8,128)(2,1)}) custom-call(bf16[256,256]{1,0:T(8,128)(2,1)} %bitcast.11, s32[27,1,256]{2,1,0:T(1,128)} %bitcast.13, s32[1,256]{1,0:T(1,128)} %parents.1, f32[1,256]{1,0:T(1,128)} %bitcast.14, f32[1,256]{1,0:T(1,128)} %bitcast.15, ...), custom_call_target="tpu_custom_call" | custom-call | tf_op jit(solution)/shard_map/pallas_call | solution.py:433
  42.0 1.9 %shard_map.113 = (bf16[256,256]{1,0:T(8,128)(2,1)}, bf16[64,512]{1,0:T(8,128)(2,1)}, f32[256,512]{1,0:T(8,128)}) custom-call(bf16[256,256]{1,0:T(8,128)(2,1)} %get-tuple-element.9.fine, bf16[64,512]{1,0:T(8,128)(2,1)} %get-tuple-element.10.coarse, bf16[32,16,256]{2,1,0:T(8,128)(2,1)} %get-tuple-element.11.gathered), custom_call_target="tpu_custom_call" | custom-call | tf_op jit(solution)/shard_map/pallas_call | solution.py:487

commit v3 on v2

--- a/solution.py
+++ b/solution.py
@@ -21,11 +21,11 @@
 
 def kernel(
     shape,
-    features,
-    neighbours,
-    parents,
-    gain_first,
-    gain_second,
+    features_hbm,
+    neighbours_hbm,
+    parents_hbm,
+    gain_first_hbm,
+    gain_second_hbm,
     first_hbm,
     second_hbm,
     down_hbm,
@@ -33,6 +33,11 @@
     fine_hbm,
     coarse_hbm,
     grad_hbm,
+    features,
+    neighbours,
+    parents,
+    gain_first,
+    gain_second,
     window,
     middle,
     select,
@@ -49,6 +54,8 @@
     tally_out,
     tally_in,
     parts,
+    swap,
+    merged,
     landed,
     gathered,
     weight_sem,
@@ -62,12 +69,15 @@
     all_send,
     all_recv,
     out_sem,
+    swap_send,
+    swap_recv,
+    input_sem,
 ):
     n_dp, n_space, taps, group, chunks, stride, scale = shape
     n = n_dp * n_space
     rows = features.shape[0]
     par = cot.shape[0] // 2
-    chunk_rows, chunk_cols = parts.shape[1:]
+    chunk_rows, chunk_cols = parts.shape[2:]
     across = cot.shape[1] // chunk_cols
     width = features.shape[1]
     me_dp, me = lax.axis_index("dp"), lax.axis_index("space")
@@ -92,16 +102,30 @@
         cut = pl.ds(g * span, span)
         return pltpu.make_async_copy(source.at[cut], target.at[cut], weight_sem.at[which, g])
 
+    inputs = [
+        pltpu.make_async_copy(source, target, input_sem.at[i])
+        for i, (source, target) in enumerate(
+            (
+                (neighbours_hbm, neighbours),
+                (parents_hbm, parents),
+                (features_hbm, features),
+                (gain_first_hbm, gain_first),
+                (gain_second_hbm, gain_second),
+            )
+        )
+    ]
     small = [
         pltpu.make_async_copy(down_hbm, down, small_sem.at[0]),
         pltpu.make_async_copy(cot_hbm, cot.at[pl.ds(0, par)], small_sem.at[1]),
     ]
-    for copy in small:
+    for copy in inputs + small:
         copy.start()
     for which in range(2):
         for g in range(steps):
             weight_copy(which, g).start()
 
+    for copy in inputs:
+        copy.wait()
     ids = neighbours[:, 0, :]
     lookup = jnp.where(ids < 0, -1, ids - (me - 1) * rows).astype(F32)
     columns = jnp.transpose(lookup)
@@ -185,6 +209,7 @@
                 halo(buffer, phase, side).wait_send()
 
     odd = me % 2
+    half = chunks // 2
 
     def convolve(buffer, weights, which):
         def pick(stage, g):
@@ -293,28 +318,51 @@
     )
     for k in range(chunks):
         r, c = (k // across) * chunk_rows, (k % across) * chunk_cols
-        parts[k] = local[r : r + chunk_rows, c : c + chunk_cols].astype(BF16)
-
-    mine = flat // stride
-    owns = flat % stride == 0
-
-    def part_copy(i):
-        k = (mine + i) % chunks
+        parts[k // half, k % half] = local[r : r + chunk_rows, c : c + chunk_cols].astype(BF16)
+
+    team = n // 2
+    spot = flat // 2
+    mine = spot // stride
+    owns = spot % stride == 0
+
+    def mate(i):
+        return place(((spot + i) % team) * 2 + odd)
+
+    def trade(source, target, slot):
+        return pltpu.make_async_remote_copy(
+            src_ref=source,
+            dst_ref=target,
+            send_sem=swap_send.at[slot],
+            recv_sem=swap_recv.at[slot],
+            device_id=place(flat + 1 - 2 * odd),
+            device_id_type=MESH,
+        )
+
+    halves = trade(parts.at[1 - odd], swap, 0)
+    halves.start()
+    sums_out[...] = partial[par:]
+
+    @pl.when(has_right)
+    def _():
+        sums_copy().start()
+
+    halves.wait()
+    merged[...] = (parts[odd].astype(F32) + swap[...].astype(F32)).astype(BF16)
+
+    def send_part(i, carry):
+        k = (mine + i) % half
         owner = k * stride
-        return owner, pltpu.make_async_remote_copy(
-            src_ref=parts.at[k],
-            dst_ref=landed.at[(flat - owner - 1 + n) % n],
+        pltpu.make_async_remote_copy(
+            src_ref=merged.at[k],
+            dst_ref=landed.at[(spot - owner - 1 + team) % team],
             send_sem=part_send,
             recv_sem=part_recv,
-            device_id=place(owner),
+            device_id=place(owner * 2 + odd),
             device_id_type=MESH,
-        )
-
-    def send_part(i, carry):
-        part_copy(i)[1].start()
+        ).start()
         return carry
 
-    lax.fori_loop(1, chunks, send_part, 0)
+    lax.fori_loop(1, half, send_part, 0)
     if stride > 1:
 
         @pl.when(jnp.logical_not(owns))
@@ -326,11 +374,8 @@
         pltpu.make_async_copy(coarse, coarse_hbm, out_sem.at[1]),
     ]
     outs[0].start()
-    sums_out[...] = partial[par:]
-
     @pl.when(has_right)
     def _():
-        sums_copy().start()
         sums_copy().wait_send()
 
     @pl.when(has_left)
@@ -348,38 +393,38 @@
             dst_ref=cut,
             send_sem=send,
             recv_sem=recv,
-            device_id=place((flat + 1) % n),
+            device_id=mate(1),
             device_id_type=MESH,
         )
 
     def share(i, carry):
         pltpu.make_async_remote_copy(
-            src_ref=gathered.at[mine],
-            dst_ref=gathered.at[mine],
+            src_ref=gathered.at[odd, mine],
+            dst_ref=gathered.at[odd, mine],
             send_sem=all_send,
             recv_sem=all_recv,
-            device_id=place((flat + i) % n),
+            device_id=mate(i),
             device_id_type=MESH,
         ).start()
         return carry
 
     def own():
-        bulk(landed, n - 1, part_send, part_recv).wait_recv()
-        mean = parts[mine].astype(F32)
+        bulk(landed, team - 1, part_send, part_recv).wait_recv()
+        mean = merged[mine].astype(F32)
 
         def add(i, running):
             return running + landed[i].astype(F32)
 
-        mean = lax.fori_loop(0, n - 1, add, mean, unroll=True)
-        gathered[mine] = (mean * scale).astype(BF16)
-        lax.fori_loop(1, n, share, 0)
-        bulk(parts, chunks - 1, part_send, part_recv).wait_send()
-        bulk(gathered, chunks - 1, all_send, all_recv).wait_recv()
-        bulk(landed, n - 1, all_send, all_recv).wait_send()
+        mean = lax.fori_loop(0, team - 1, add, mean, unroll=True)
+        gathered[odd, mine] = (mean * scale).astype(BF16)
+        lax.fori_loop(1, team, share, 0)
+        bulk(merged, half - 1, part_send, part_recv).wait_send()
+        bulk(gathered.at[odd], half - 1, all_send, all_recv).wait_recv()
+        bulk(landed, team - 1, all_send, all_recv).wait_send()
 
     def follow():
-        bulk(parts, chunks, part_send, part_recv).wait_send()
-        bulk(gathered, chunks, all_send, all_recv).wait_recv()
+        bulk(merged, half, part_send, part_recv).wait_send()
+        bulk(gathered.at[odd], half, all_send, all_recv).wait_recv()
 
     if stride == 1:
         own()
@@ -387,6 +432,9 @@
         pl.when(owns)(own)
         pl.when(jnp.logical_not(owns))(follow)
 
+    whole = trade(gathered.at[odd], gathered.at[odd], 1)
+    whole.start()
+    whole.wait()
     last = pltpu.make_async_copy(gathered, grad_hbm, out_sem.at[2])
     last.start()
     for copy in outs:
@@ -395,13 +443,13 @@
 
 
 def finish(fine, coarse, gathered, fine_out, coarse_out, grad):
-    chunks, chunk_rows, chunk_cols = gathered.shape
+    _, half, chunk_rows, chunk_cols = gathered.shape
     across = grad.shape[1] // chunk_cols
     fine_out[...] = fine[...]
     coarse_out[...] = coarse[...]
-    for k in range(chunks):
+    for k in range(2 * half):
         r, c = (k // across) * chunk_rows, (k % across) * chunk_cols
-        grad[r : r + chunk_rows, c : c + chunk_cols] = gathered[k].astype(F32)
+        grad[r : r + chunk_rows, c : c + chunk_cols] = gathered[k // half, k % half].astype(F32)
 
 
 def body(
@@ -435,11 +483,16 @@
         out_shape=(
             jax.ShapeDtypeStruct((rows, width), BF16),
             jax.ShapeDtypeStruct((par, out_width), BF16),
-            jax.ShapeDtypeStruct((chunks, chunk_rows, chunk_cols), BF16),
+            jax.ShapeDtypeStruct((2, chunks // 2, chunk_rows, chunk_cols), BF16),
         ),
-        in_specs=[vmem] * 5 + [hbm] * 4,
+        in_specs=[hbm] * 9,
         out_specs=(hbm,) * 3,
         scratch_shapes=[
+            pltpu.VMEM((rows, width), BF16),
+            pltpu.VMEM((taps, 1, rows), jnp.int32),
+            pltpu.VMEM((1, rows), jnp.int32),
+            pltpu.VMEM((1, width), F32),
+            pltpu.VMEM((1, width), F32),
             pltpu.VMEM((3 * rows, width), BF16),
             pltpu.VMEM((3 * rows, width), BF16),
             pltpu.VMEM((taps, rows, 3 * rows), BF16),
@@ -455,9 +508,11 @@
             pltpu.VMEM((par, width), F32),
             pltpu.VMEM((2 * par, 128), F32),
             pltpu.VMEM((2 * par, 128), F32),
-            pltpu.VMEM((chunks, chunk_rows, chunk_cols), BF16),
-            pltpu.VMEM((n - 1, chunk_rows, chunk_cols), BF16),
-            pltpu.VMEM((chunks, chunk_rows, chunk_cols), BF16),
+            pltpu.VMEM((2, chunks // 2, chunk_rows, chunk_cols), BF16),
+            pltpu.VMEM((chunks // 2, chunk_rows, chunk_cols), BF16),
+            pltpu.VMEM((chunks // 2, chunk_rows, chunk_cols), BF16),
+            pltpu.VMEM((n // 2 - 1, chunk_rows, chunk_cols), BF16),
+            pltpu.VMEM((2, chunks // 2, chunk_rows, chunk_cols), BF16),
             dma((2, taps // group)),
             dma((2,)),
             dma((2, 2)),
@@ -469,6 +524,9 @@
             dma,
             dma,
             dma((3,)),
+            dma((2,)),
+            dma((2,)),
+            dma((5,)),
         ],
         compiler_params=pltpu.CompilerParams(
             collective_id=0, has_side_effects=True, vmem_limit_bytes=60 * 2**20

time: 44.1 us -> 41.5 us (0.941)
  Pallas kernels: 43.3 us -> 40.7 us
    pallas_call x1, Pallas kernels: 41.3 us -> 38.8 us  [body(): pl.pallas_call(functools.partial(kernel, (n_dp, n_space, taps, group, chu...]
where the time goes in v3:
time: 41.5 us; the launch traced here: 41.4 us
  Pallas kernels  40.7 us (98%)
  between operations  0.64 us (2%)
    pallas_call x1, Pallas kernels, body(): pl.pallas_call(functools.partial(kernel, (n_dp, n_space, taps, group, chu...  38.8 us
    pallas_call x1, Pallas kernels, body(): pl.pallas_call(finish, out_shape=(jax.ShapeDtypeStruct((rows, width), BF1...  1.92 us

profile of v3, /device:TPU:0, one launch (start us, length us, event | category | flops | bytes accessed | tf_op | source)
XLA Modules:
  0.0 41.4 jit_solution(5652267435357039866)
XLA Ops:
  0.6 38.8 %shard_map.112 = (bf16[256,256]{1,0:T(8,128)(2,1)}, bf16[64,512]{1,0:T(8,128)(2,1)}, bf16[2,16,16,256]{3,2,1,0:T(8,128)(2,1)}) custom-call(bf16[256,256]{1,0:T(8,128)(2,1)} %bitcast.11, s32[27,1,256]{2,1,0:T(1,128)} %bitcast.13, s32[1,256]{1,0:T(1,128)} %parents_hbm.1, f32[1,256]{1,0:T(1,128)} %bitcast.14, f32[1,256]{1,0:T(1,128)} %bitcast.15, ...), custom_call_target="tpu_custom_call" | custom-call | tf_op jit(solution)/shard_map/pallas_call | solution.py:481
  39.5 1.9 %shard_map.113 = (bf16[256,256]{1,0:T(8,128)(2,1)}, bf16[64,512]{1,0:T(8,128)(2,1)}, f32[256,512]{1,0:T(8,128)}) custom-call(bf16[256,256]{1,0:T(8,128)(2,1)} %get-tuple-element.9.fine, bf16[64,512]{1,0:T(8,128)(2,1)} %get-tuple-element.10.coarse, bf16[2,16,16,256]{3,2,1,0:T(8,128)(2,1)} %get-tuple-element.11.gathered), custom_call_target="tpu_custom_call" | custom-call | tf_op jit(solution)/shard_map/pallas_call | solution.py:545
